TPU v7x, 256 devices: a whole 4x4x8 slice. The times are simulated.
256 devices in a mesh: sec: 2 (over y_lo), grp: 16 (over z, y_hi), tp: 8 (over x, core).
Axes of the slice: x: 4, y: 4 (y_hi: 2, y_lo: 2; y = y_hi * 2 + y_lo), z: 8, core: 2. Of those that a mesh axis runs over, the one named last changes fastest.
Arguments:
- hidden_in: bfloat16 [1024, 7168], P(('sec', 'grp', 'tp')), may hold values from -6 to 6
- queries: bfloat16 [1024, 16, 8, 576], P(('sec', 'grp'), None, 'tp'), may hold values from -61 to 61
- latent_cache: bfloat16 [1024, 64, 576], P(('sec', 'grp')), may hold values from -6 to 6
- lengths: int32 [1024], P(('sec', 'grp')), may hold values from 2 to 64, as said below
- w_uv: bfloat16 [16, 8, 512, 128], P(None, 'tp'), may hold values from -0.75 to 0.75
- attn_weight: bfloat16 [16, 8, 128, 7168], P(None, 'tp', None, 'grp'), may hold values from -0.125 to 0.125
- norm_gain: float32 [7168], replicated, may hold values from 0.1 to 1.9
- router: bfloat16 [7168, 32], replicated, may hold values from -0.0625 to 0.0625
- routes: int32 [1024, 8], P(('sec', 'grp', 'tp')), may hold values from 0 to 31, all different within a row; in each aligned block of 4 rows (0 to 3, 4 to 7, ...) at most 2 rows name the same one
- live_counts: int32 [256], P(('sec', 'grp', 'tp')), may hold values from 3 to 4, as said below
- expert_in: bfloat16 [32, 7168, 2, 1024], P(('sec', 'grp'), None, None, 'tp'), may hold values from -0.0625 to 0.0625
- expert_out: bfloat16 [32, 1024, 7168], P(('sec', 'grp'), 'tp'), may hold values from -0.5 to 0.5
Outputs:
- layer_out: bfloat16 [1024, 7168], P(('sec', 'grp', 'tp'))
Inputs may be any that keep to these rules, and one draw needn't show every extreme that they name: `lengths`: some request has exactly 64 cached positions and some has 2. `live_counts`: some device has all 4 slots live and some has exactly 3. `routes`: the 8 experts of a token differ. Within the rows of one device (aligned blocks of 4 rows) no expert is named by more than 2 rows, a bound that some block reaches.
All inputs are finite; a program needn't handle non-finite values.
Results may differ from a plain program's by a relative error of at most 0.018.
Values may be sent and summed in bfloat16 or wider, within the bound.
No kernel may reach another device: no remote copies, remote signals or barrier semaphores. Data moves between devices by JAX's collectives and lax.ppermute only.
A program may use at most 64 MiB of HBM per device.

v0:
```python
import jax
import jax.numpy as jnp
from jax import lax
from jax.sharding import Mesh
from jax.sharding import PartitionSpec as P


GRP = ("grp_0", "grp_1")
SEC_GRP = ("sec", "grp_0", "grp_1")
TP = ("x", "core")
GRP_TP = ("grp_0", "grp_1", "x", "core")
SEC_GRP_TP = ("sec", "grp_0", "grp_1", "x", "core")


score_scale = 192.0 ** (-0.5)
route_scale = 2.5


def shifted(x, axis, step):
    size = lax.axis_size(axis)
    return lax.ppermute(x, axis, [(i, (i + step) % size) for i in range(size)])


def rolled(blocks, count):
    size = blocks.shape[0]
    return lax.dynamic_slice_in_dim(jnp.concatenate([blocks, blocks]), size - count, size, 0)


def around_the_ring(block):
    middle = block.shape[0] // 2
    before = {step: shifted(block, "grp_0", step) for step in (1, 2)}
    after = {step: shifted(block, "grp_0", -step) for step in (1, 2)}
    before[3] = shifted(before[2], "grp_0", 1)
    after[3] = shifted(after[2], "grp_0", -1)
    far = jnp.concatenate(
        [shifted(before[2][:middle], "grp_0", 2), shifted(after[2][middle:], "grp_0", -2)]
    )
    near = [block, after[1], after[2], before[2], before[1]]
    return near, [after[3], far, before[3]]


def projected(head_rows, out_block):
    rows, columns = head_rows.shape[0], out_block.shape[1]
    partner = shifted(head_rows, "grp_1", 1)
    products = []
    for gathered in zip(around_the_ring(head_rows), around_the_ring(partner)):
        product = jnp.dot(
            jnp.concatenate(gathered[0] + gathered[1]), out_block, preferred_element_type=jnp.float32
        ).astype(jnp.bfloat16)
        products.append(product.reshape(2, len(gathered[0]), rows, columns))
    near, far = products
    places = jnp.concatenate([near[:, :3], far, near[:, 3:]], axis=1)
    places = rolled(places, lax.axis_index("grp_1"))
    return rolled(jnp.moveaxis(places, 1, 0), lax.axis_index("grp_0"))


def rolled(blocks, count):
    size = blocks.shape[0]
    return lax.dynamic_slice_in_dim(jnp.concatenate([blocks, blocks]), size - count, size, 0)


def own_and_other(array, core, dim):
    size = array.shape[dim] // 2
    return [lax.dynamic_slice_in_dim(array, number * size, size, dim) for number in (core, 1 - core)]


def around_the_ring(block):
    middle = block.shape[0] // 2
    before = {step: shifted(block, "grp_0", step) for step in (2, 1)}
    after = {step: shifted(block, "grp_0", -step) for step in (2, 1)}
    before[3] = shifted(before[2], "grp_0", 1)
    after[3] = shifted(after[2], "grp_0", -1)
    opposite = jnp.concatenate(
        [shifted(before[2][:middle], "grp_0", 2), shifted(after[2][middle:], "grp_0", -2)]
    )
    return [block, after[1], after[2], before[2], before[1]], [after[3], opposite, before[3]]


def projected(head_rows, out_block):
    rows, columns = head_rows.shape[0], out_block.shape[1]
    partner = shifted(head_rows, "grp_1", 1)
    products = []
    for gathered in around_the_ring(jnp.concatenate([head_rows, partner])):
        product = jnp.dot(
            jnp.concatenate(gathered), out_block, preferred_element_type=jnp.float32
        ).astype(jnp.bfloat16)
        product = jnp.pad(product, ((0, 0), (0, -columns % 128)))
        products.append(product.reshape(len(gathered), 2, rows, -1))
    near, far = products
    places = jnp.concatenate([near[:3], far, near[3:]])
    places = rolled(jnp.moveaxis(places, 1, 0), lax.axis_index("grp_1"))
    return rolled(jnp.moveaxis(places, 0, 1), lax.axis_index("grp_0"))


def attention_rows(queries, latent_cache, lengths, w_uv):
    latent_width = w_uv.shape[2]
    query_block = queries[:, :, 0, :]
    scores = (
        jnp.einsum("bhr,bpr->bhp", query_block, latent_cache, preferred_element_type=jnp.float32)
        * score_scale
    )
    positions = jnp.arange(latent_cache.shape[1])
    visible = positions[None, None, :] < lengths[:, None, None]
    scores = jnp.where(visible, scores, -1e30)
    highest = jnp.max(scores, axis=2, keepdims=True)
    raised = jnp.exp(scores - highest)
    softmax_weights = (raised / jnp.sum(raised, axis=2, keepdims=True)).astype(jnp.bfloat16)
    latent_out = jnp.einsum(
        "bhp,bpc->bhc",
        softmax_weights,
        latent_cache[:, :, :latent_width],
        preferred_element_type=jnp.float32,
    ).astype(jnp.bfloat16)
    head_out = jnp.einsum(
        "bhc,hcv->bhv", latent_out, w_uv[:, 0], preferred_element_type=jnp.float32
    ).astype(jnp.bfloat16)
    return head_out.reshape(head_out.shape[0], -1)


def layer(
    hidden_in,
    queries,
    latent_cache,
    lengths,
    w_uv,
    attn_weight,
    norm_gain,
    router,
    routes,
    live_counts,
    expert_in,
    expert_out,
):
    count_of_tokens, width = hidden_in.shape
    groups = lax.axis_size(GRP)
    slices = lax.axis_size(TP)
    chips = lax.axis_size("x")
    chip, core = lax.axis_index("x"), lax.axis_index("core")
    part = width // slices
    slice_width = expert_in.shape[3]

    head_rows = attention_rows(queries, latent_cache, lengths, w_uv)
    head_rows, expert_in = lax.optimization_barrier((head_rows, expert_in))

    rows_of_chip = width // chips
    in_parts = [
        lax.dynamic_slice_in_dim(expert_in[0], (chip + step) % chips * rows_of_chip, rows_of_chip, 0)
        for step in range(chips)
    ]
    in_parts[1:] = [shifted(in_parts[step], "x", step) for step in range(1, chips)]

    out_block = attn_weight[:, 0].reshape(-1, attn_weight.shape[3])
    partial_value = projected(head_rows, out_block)
    partial_value = partial_value.reshape(groups * slices, count_of_tokens, -1)
    partial_value, expert_out = lax.optimization_barrier((partial_value, expert_out))
    in_parts, _ = lax.optimization_barrier((in_parts, partial_value))
    in_columns = jnp.concatenate(
        [p.reshape(rows_of_chip, 2 * slice_width) for p in in_parts], axis=1
    )
    arrived = lax.all_to_all(partial_value, GRP_TP, split_axis=0, concat_axis=0, tiled=True)
    out_parts = [
        lax.dynamic_slice_in_dim(expert_out[0], (chip + step) % chips * rows_of_chip, rows_of_chip, 1)
        for step in range(chips)
    ]
    out_parts[1:] = [shifted(out_parts[step], "x", step) for step in range(1, chips)]
    arrived = arrived[:, :, : attn_weight.shape[3]]
    summed = arrived.reshape(groups, slices, count_of_tokens, -1).astype(jnp.float32).sum(axis=1)
    attention = jnp.moveaxis(summed.astype(jnp.bfloat16), 0, 1).reshape(count_of_tokens, width)

    residual = hidden_in.astype(jnp.float32) + attention.astype(jnp.float32)
    normalized_input = (
        residual
        * lax.rsqrt(jnp.mean(residual * residual, axis=1, keepdims=True) + 1e-06)
        * norm_gain
    ).astype(jnp.bfloat16)
    experts = router.shape[1]
    per_token = routes.shape[1]
    capacity = max(2, 2 * count_of_tokens * per_token // experts)
    picked = routes[:, :, None] == jnp.arange(experts)[None, None, :]
    living = jnp.arange(count_of_tokens) < live_counts[0]
    routed = jnp.any(picked, axis=1) & living[:, None]
    routed_count = routed.astype(jnp.int32)
    slot_index = jnp.cumsum(routed_count, axis=0) - routed_count
    placed_tokens = routed[:, :, None] & (
        slot_index[:, :, None] == jnp.arange(capacity)[None, None, :]
    )
    outgoing = jnp.einsum(
        "poy,ptj->otyj",
        placed_tokens.astype(jnp.bfloat16),
        normalized_input.reshape(count_of_tokens, slices, part),
        preferred_element_type=jnp.float32,
    ).astype(jnp.bfloat16)
    outgoing = outgoing.reshape(experts * slices, capacity, part)
    outgoing, in_columns = lax.optimization_barrier((outgoing, in_columns))
    in_own, in_other = own_and_other(in_columns, core, 0)
    arrived_rows = lax.all_to_all(
        outgoing, SEC_GRP_TP, split_axis=0, concat_axis=0, tiled=True
    )

    rows = arrived_rows.reshape(-1, part)
    other_rows = shifted(rows, "core", 1)
    products = jnp.dot(rows, in_own, preferred_element_type=jnp.float32) + jnp.dot(
        other_rows, in_other, preferred_element_type=jnp.float32
    )
    products = jnp.split(products, chips, axis=1)
    sent = {step: products[step].astype(jnp.bfloat16) for step in (2, 1, 3)}
    gate_up = products[0]
    for step, block in sent.items():
        gate_up = gate_up + shifted(block, "x", -step).astype(jnp.float32)
    out_parts, _ = lax.optimization_barrier((out_parts, sent[1]))
    out_own, out_sent = own_and_other(jnp.concatenate(out_parts), core, 1)
    out_other = shifted(out_sent, "core", 1)
    activated = (jax.nn.silu(gate_up[:, :slice_width]) * gate_up[:, slice_width:]).astype(
        jnp.bfloat16
    )
    hidden_own = jnp.concatenate(
        [activated] + [shifted(activated, "x", step) for step in range(1, chips)], axis=1
    )
    hidden_other = shifted(hidden_own, "core", 1)
    values = (
        jnp.dot(hidden_own, out_own, preferred_element_type=jnp.float32)
        + jnp.dot(hidden_other, out_other, preferred_element_type=jnp.float32)
    ).astype(jnp.bfloat16)
    values = values.reshape(experts * slices, capacity, part)
    back = lax.all_to_all(values, SEC_GRP_TP, split_axis=0, concat_axis=0, tiled=True)
    back = back.reshape(experts, slices, capacity, part)

    placed_late, _ = lax.optimization_barrier((placed_tokens, values))
    logits = jnp.dot(normalized_input, router, preferred_element_type=jnp.float32)
    affinity = jax.nn.sigmoid(logits)
    chosen = jnp.sum(jnp.where(picked, affinity[:, None, :], 0.0), axis=2)
    gate_weights = (
        route_scale
        * chosen
        / jnp.sum(chosen, axis=1, keepdims=True)
        * living[:, None].astype(jnp.float32)
    )
    expert_gate = jnp.sum(jnp.where(picked, gate_weights[:, :, None], 0.0), axis=1)
    combine_rows = placed_late.astype(jnp.float32) * expert_gate[:, :, None]

    coarse = lax.reduce_precision(combine_rows, 8, 7)
    weights = jnp.concatenate([coarse, combine_rows - coarse], axis=0).astype(jnp.bfloat16)
    mixed = jnp.einsum("poy,otyj->ptj", weights, back, preferred_element_type=jnp.float32)
    expert_mix = (mixed[:count_of_tokens] + mixed[count_of_tokens:]).reshape(count_of_tokens, width)
    return (residual + expert_mix).astype(jnp.bfloat16)


def solution(mesh):
    torus = Mesh(
        mesh.devices.reshape(mesh.shape["sec"], 8, 2, mesh.shape["tp"] // 2, 2), SEC_GRP_TP
    )
    in_specs = (
        P(SEC_GRP_TP, None),
        P(SEC_GRP, None, TP, None),
        P(SEC_GRP, None, None),
        P(SEC_GRP),
        P(None, TP, None, None),
        P(None, TP, None, GRP),
        P(),
        P(),
        P(SEC_GRP_TP, None),
        P(SEC_GRP_TP),
        P(SEC_GRP, None, None, TP),
        P(SEC_GRP, TP, None),
    )
    out_specs = P(SEC_GRP_TP, None)
    return jax.shard_map(layer, mesh=torus, in_specs=in_specs, out_specs=out_specs, check_vma=False)
```

profile of v0, /device:TPU:8, one launch (start us, length us, event | category | flops | bytes accessed | tf_op | source)
XLA Modules:
  0.0 222.5 jit_solution(3171244867641570983)
XLA Ops:
  0.9 2.9 %fusion.30 = f32[32,16,64]{2,1,0:T(8,128)S(1)} fusion(bf16[32,64,576]{2,1,0:T(8,128)(2,1)} %param.14, bf16[32,16,1,576]{3,1,2,0:T(8,128)(2,1)} %param.13, pred[32,64]{1,0:T(8,128)(4,1)S(1)} %iota_compare_fusion.1), kind=kOutput, calls=%fused_computation.26 | convolution fusion | flops 37814272 | bytes 3082240 | tf_op jit(solution)/shard_map/bhr,bpr->bhp/dot_general | solution.py:99
  4.0 2.5 %fusion.19 = bf16[32,16,512]{2,1,0:T(8,128)(2,1)S(1)} fusion(bf16[32,64,576]{2,1,0:T(8,128)(2,1)} %param.14, f32[32,16]{1,0:T(8,128)S(1)} %fusion.73, f32[32,16,64]{2,1,0:T(8,128)S(1)} %fusion.30), kind=kOutput, calls=%fused_computation.20 | convolution fusion | flops 33915456 | bytes 3162112 | tf_op jit(solution)/shard_map/bhp,bpc->bhc/dot_general | solution.py:108
  7.2 4.9 %dynamic-slice_bitcast_fusion = (bf16[1792,2,128]{2,1,0:T(2,128)(2,1)}, bf16[1792,2,128]{2,1,0:T(2,128)(2,1)}, bf16[1792,2,128]{2,1,0:T(2,128)(2,1)}, bf16[1792,2,128]{2,1,0:T(2,128)(2,1)S(1)}) fusion(bf16[1,7168,2,128]{3,2,1,0:T(2,128)(2,1)} %param.22, s32[]{:T(128)S(6)} %select_n.79, s32[]{:T(128)S(6)} %select_n.77, s32[]{:T(128)S(6)} %select_n.75, ...), kind=kLoop, calls=%fused_computation.45 | loop fusion | bytes 7340048 | tf_op jit(solution)/shard_map/dynamic_slice | solution.py:147
  12.2 3.0 %collective-permute-start.10 = (bf16[1792,2,128]{2,1,0:T(2,128)(2,1)}, bf16[1792,2,128]{2,1,0:T(2,128)(2,1)}, u32[]{:S(2)}, u32[]{:S(2)}) collective-permute-start(bf16[1792,2,128]{2,1,0:T(2,128)(2,1)} %get-tuple-element.40), channel_id=1, source_target_pairs={{0,4},{2,6},{4,0},{6,2},{1,5},{3,7},{5,1},{7,3},{8,12},{10,14},{12... | collective-permute-start | bytes 2752520 | tf_op jit(solution)/shard_map/ppermute | solution.py:21
  15.2 2.3 %collective-permute-start = (bf16[32,2048]{1,0:T(8,128)(2,1)S(1)}, bf16[32,2048]{1,0:T(8,128)(2,1)S(1)}, u32[]{:S(2)}, u32[]{:S(2)}) collective-permute-start(bf16[32,2048]{1,0:T(8,128)(2,1)S(1)} %bitcast.111), channel_id=1, source_target_pairs={{0,8},{8,0},{1,9},{9,1},{2,10},{10,2},{3,11},{11,3},{4,12},{12,4},... | collective-permute-start | bytes 393224 | tf_op jit(solution)/shard_map/ppermute | solution.py:21
  19.6 2.0 collective-permute-done
  22.4 5.9 %collective-permute-start.1 = (bf16[64,2048]{1,0:T(8,128)(2,1)}, bf16[64,2048]{1,0:T(8,128)(2,1)}, u32[]{:S(2)}, u32[]{:S(2)}) collective-permute-start(bf16[64,2048]{1,0:T(8,128)(2,1)} %get-tuple-element.50), channel_id=1, source_target_pairs={{0,112},{16,0},{32,16},{48,32},{64,48},{80,64},{96,80},{112,96},{1... | collective-permute-start | bytes 786440 | tf_op jit(solution)/shard_map/ppermute | solution.py:21
  28.3 1.4 collective-permute-start.2
  29.7 1.5 collective-permute-start.3
  31.2 3.9 %copy.47 = bf16[16,1,128,448]{2,0,3,1:T(8,128)(2,1)} copy(bf16[16,1,128,448]{2,3,1,0:T(8,128)(2,1)} %param.17) | data formatting | bytes 3670016 | tf_op args[5]
  35.2 9.8 %collective-permute-done.3 = bf16[64,2048]{1,0:T(8,128)(2,1)S(1)} collective-permute-done((bf16[64,2048]{1,0:T(8,128)(2,1)}, bf16[64,2048]{1,0:T(8,128)(2,1)S(1)}, u32[]{:S(2)}, u32[]{:S(2)}) %collective-permute-start.3) | collective-permute-done | bytes 262176 | tf_op jit(solution)/shard_map/ppermute | solution.py:21
  45.9 3.5 %collective-permute-start.7 = (bf16[32,2048]{1,0:T(8,128)(2,1)S(1)}, bf16[32,2048]{1,0:T(8,128)(2,1)S(1)}, u32[]{:S(2)}, u32[]{:S(2)}) collective-permute-start(bf16[32,2048]{1,0:T(8,128)(2,1)S(1)} %slice.49), channel_id=1, source_target_pairs={{0,96},{16,112},{32,0},{48,16},{64,32},{80,48},{96,64},{112,80},{1... | collective-permute-start | bytes 393224 | tf_op jit(solution)/shard_map/ppermute | solution.py:21
  49.8 1.7 constant_dynamic-update-slice_fusion.5
  53.0 1.6 collective-permute-start.8
  55.3 2.2 fusion.22
  57.5 1.2 collective-permute-start.11
  58.7 0.9 collective-permute-start.9
  61.8 0.9 reshape.192
  62.7 8.3 %all-to-all-start = ((bf16[128,4,512]{2,1,0:T(4,128)(2,1)}), bf16[128,4,512]{2,1,0:T(4,128)(2,1)S(1)}, u32[]{:S(2)}, u32[]{:S(2)}) async-start(bf16[128,4,512]{2,1,0:T(4,128)(2,1)} %reshape.192), calls=%async_computation | async-start | bytes 1048576 | tf_op jit(solution)/shard_map/all_to_all | solution.py:160
  71.0 8.8 %collective-permute-done.11 = bf16[1792,2,128]{2,1,0:T(2,128)(2,1)} collective-permute-done((bf16[1792,2,128]{2,1,0:T(2,128)(2,1)}, bf16[1792,2,128]{2,1,0:T(2,128)(2,1)}, u32[]{:S(2)}, u32[]{:S(2)}) %collective-permute-start.11) | collective-permute-done | bytes 917536 | tf_op jit(solution)/shard_map/ppermute | solution.py:21
  79.8 2.9 %collective-permute-done.9 = bf16[1792,2,128]{2,1,0:T(2,128)(2,1)} collective-permute-done((bf16[1792,2,128]{2,1,0:T(2,128)(2,1)}, bf16[1792,2,128]{2,1,0:T(2,128)(2,1)}, u32[]{:S(2)}, u32[]{:S(2)}) %collective-permute-start.9) | collective-permute-done | bytes 917536 | tf_op jit(solution)/shard_map/ppermute | solution.py:21
  82.7 1.5 copy_bitcast_fusion.2
  84.2 1.7 copy_bitcast_fusion
  86.0 2.1 pad_maximum_fusion
  88.0 3.0 %all-to-all-done = bf16[128,4,512]{2,1,0:T(4,128)(2,1)S(1)} async-done(((bf16[128,4,512]{2,1,0:T(4,128)(2,1)}), bf16[128,4,512]{2,1,0:T(4,128)(2,1)S(1)}, u32[]{:S(2)}, u32[]{:S(2)}) %all-to-all-start) | async-done | bytes 524320 | tf_op jit(solution)/shard_map/all_to_all | solution.py:160
  92.8 0.9 copy.51
  93.7 33.9 %all_to_all.15 = bf16[256,2,896]{2,1,0:T(2,128)(2,1)S(1)} all-to-all(bf16[256,2,896]{2,1,0:T(2,128)(2,1)S(1)} %copy.51), channel_id=1, replica_groups=mesh['sec'=2,'grp_0'=8,'grp_1'=2,'x'=4,'core'=2] {'sec','grp_0','grp_1',..., dimensions={0} | all-to-all | bytes 1835008 | tf_op jit(solution)/shard_map/all_to_all | solution.py:196
  127.6 1.3 reshape.200
  128.9 1.7 dynamic-slice_bitcast_fusion.4
  131.3 1.3 collective-permute-start.20
  132.6 1.7 collective-permute-start.21
  134.3 2.4 %fusion.11 = f32[512,1024]{1,0:T(8,128)S(1)} fusion(bf16[512,896]{1,0:T(8,128)(2,1)} %reshape.200, bf16[1792,1024]{1,0:T(8,128)(2,1)S(1)} %copy-done.1, s32[]{:T(128)S(6)} %select_n.80), kind=kOutput, calls=%fused_computation.13 | convolution fusion | flops 939524096 | bytes 4849668 | tf_op jit(solution)/shard_map/dot_general | solution.py:202
  136.8 1.3 fusion.74
  138.1 1.2 collective-permute-start.14
  139.3 15.4 %collective-permute-done.19 = bf16[128,1792]{1,0:T(8,128)(2,1)S(1)} collective-permute-done((bf16[128,1792]{1,0:T(8,128)(2,1)S(1)}, bf16[128,1792]{1,0:T(8,128)(2,1)S(1)}, u32[]{:S(2)}, u32[]{:S(2)}) %collective-permute-start.19) | collective-permute-done | bytes 458784 | tf_op jit(solution)/shard_map/ppermute | solution.py:21
  154.7 1.4 collective-permute-done.21
  156.1 1.0 collective-permute-start.13
  157.1 1.9 collective-permute-start.15
  159.3 7.5 %collective-permute-done.13 = bf16[512,256]{1,0:T(8,128)(2,1)S(1)} collective-permute-done((bf16[512,256]{1,0:T(8,128)(2,1)S(1)}, bf16[512,256]{1,0:T(8,128)(2,1)S(1)}, u32[]{:S(2)}, u32[]{:S(2)}) %collective-permute-start.13) | collective-permute-done | bytes 262176 | tf_op jit(solution)/shard_map/ppermute | solution.py:21
  166.8 3.3 %collective-permute-done.15 = bf16[512,256]{1,0:T(8,128)(2,1)S(1)} collective-permute-done((bf16[512,256]{1,0:T(8,128)(2,1)S(1)}, bf16[512,256]{1,0:T(8,128)(2,1)S(1)}, u32[]{:S(2)}, u32[]{:S(2)}) %collective-permute-start.15) | collective-permute-done | bytes 262176 | tf_op jit(solution)/shard_map/ppermute | solution.py:21
  170.5 2.1 collective-permute-start.17
  172.5 1.4 collective-permute-start.18
  173.9 6.0 %collective-permute-done.16 = bf16[512,128]{1,0:T(8,128)(2,1)S(1)} collective-permute-done((bf16[512,128]{1,0:T(8,128)(2,1)S(1)}, bf16[512,128]{1,0:T(8,128)(2,1)S(1)}, u32[]{:S(2)}, u32[]{:S(2)}) %collective-permute-start.16) | collective-permute-done | bytes 131104 | tf_op jit(solution)/shard_map/ppermute | solution.py:21
  180.7 1.9 collective-permute-done.22
  184.0 1.3 reshape.201
  185.3 8.4 %all-to-all-start.2 = ((bf16[256,2,896]{2,1,0:T(2,128)(2,1)}), bf16[256,2,896]{2,1,0:T(2,128)(2,1)S(1)}, u32[]{:S(2)}, u32[]{:S(2)}) async-start(bf16[256,2,896]{2,1,0:T(2,128)(2,1)} %reshape.201), calls=%async_computation.2 | async-start | bytes 1835008 | tf_op jit(solution)/shard_map/all_to_all | solution.py:225
  193.7 1.2 fusion.39
  195.4 26.1 %all-to-all-done.2 = bf16[256,2,896]{2,1,0:T(2,128)(2,1)S(1)} async-done(((bf16[256,2,896]{2,1,0:T(2,128)(2,1)}), bf16[256,2,896]{2,1,0:T(2,128)(2,1)S(1)}, u32[]{:S(2)}, u32[]{:S(2)}) %all-to-all-start.2) | async-done | bytes 917536 | tf_op jit(solution)/shard_map/all_to_all | solution.py:225
  (89 shorter events, 16.3 us)
Async XLA Ops:
  0.0 6.5 %copy-start = (bf16[16,1,512,128]{3,2,1,0:T(8,128)(2,1)S(1)}, bf16[16,1,512,128]{3,2,1,0:T(8,128)(2,1)}, u32[]{:S(2)}) copy-start(bf16[16,1,512,128]{3,2,1,0:T(8,128)(2,1)} %param.16) | copy-start | bytes 6291460
  7.2 11.4 %copy-start.6 = (s32[4,8]{1,0:T(4,128)S(1)}, s32[4,8]{1,0:T(4,128)}, u32[]{:S(2)}) copy-start(s32[4,8]{1,0:T(4,128)} %param.20) | copy-start | bytes 388
  12.2 58.9 %collective-permute-start.10 = (bf16[1792,2,128]{2,1,0:T(2,128)(2,1)}, bf16[1792,2,128]{2,1,0:T(2,128)(2,1)}, u32[]{:S(2)}, u32[]{:S(2)}) collective-permute-start(bf16[1792,2,128]{2,1,0:T(2,128)(2,1)} %get-tuple-element.40), channel_id=1, source_target_pairs={{0,4},{2,6},{4,0},{6,2},{1,5},{3,7},{5,1},{7,3},{8,12},{10,14},{12... | collective-permute-start | bytes 2752520 | tf_op jit(solution)/shard_map/ppermute | solution.py:21
  15.2 6.5 %collective-permute-start = (bf16[32,2048]{1,0:T(8,128)(2,1)S(1)}, bf16[32,2048]{1,0:T(8,128)(2,1)S(1)}, u32[]{:S(2)}, u32[]{:S(2)}) collective-permute-start(bf16[32,2048]{1,0:T(8,128)(2,1)S(1)} %bitcast.111), channel_id=1, source_target_pairs={{0,8},{8,0},{1,9},{9,1},{2,10},{10,2},{3,11},{11,3},{4,12},{12,4},... | collective-permute-start | bytes 393224 | tf_op jit(solution)/shard_map/ppermute | solution.py:21
  22.4 27.0 %collective-permute-start.1 = (bf16[64,2048]{1,0:T(8,128)(2,1)}, bf16[64,2048]{1,0:T(8,128)(2,1)}, u32[]{:S(2)}, u32[]{:S(2)}) collective-permute-start(bf16[64,2048]{1,0:T(8,128)(2,1)} %get-tuple-element.50), channel_id=1, source_target_pairs={{0,112},{16,0},{32,16},{48,32},{64,48},{80,64},{96,80},{112,96},{1... | collective-permute-start | bytes 786440 | tf_op jit(solution)/shard_map/ppermute | solution.py:21
  28.3 17.7 %collective-permute-start.2 = (bf16[64,2048]{1,0:T(8,128)(2,1)}, bf16[64,2048]{1,0:T(8,128)(2,1)S(1)}, u32[]{:S(2)}, u32[]{:S(2)}) collective-permute-start(bf16[64,2048]{1,0:T(8,128)(2,1)} %get-tuple-element.50), channel_id=1, source_target_pairs={{0,96},{16,112},{32,0},{48,16},{64,32},{80,48},{96,64},{112,80},{1... | collective-permute-start | bytes 786440 | tf_op jit(solution)/shard_map/ppermute | solution.py:21
  29.7 15.4 %collective-permute-start.3 = (bf16[64,2048]{1,0:T(8,128)(2,1)}, bf16[64,2048]{1,0:T(8,128)(2,1)S(1)}, u32[]{:S(2)}, u32[]{:S(2)}) collective-permute-start(bf16[64,2048]{1,0:T(8,128)(2,1)} %get-tuple-element.50), channel_id=1, source_target_pairs={{0,32},{16,48},{32,64},{48,80},{64,96},{80,112},{96,0},{112,16},{1... | collective-permute-start | bytes 786440 | tf_op jit(solution)/shard_map/ppermute | solution.py:21
  35.1 20.2 %copy-start.2 = (bf16[16,1,128,448]{2,0,3,1:T(8,128)(2,1)S(1)}, bf16[16,1,128,448]{2,0,3,1:T(8,128)(2,1)}, u32[]{:S(2)}) copy-start(bf16[16,1,128,448]{2,0,3,1:T(8,128)(2,1)} %copy.47) | copy-start | bytes 5505028
  35.2 17.8 %collective-permute-start.4 = (bf16[64,2048]{1,0:T(8,128)(2,1)}, bf16[64,2048]{1,0:T(8,128)(2,1)S(1)}, u32[]{:S(2)}, u32[]{:S(2)}) collective-permute-start(bf16[64,2048]{1,0:T(8,128)(2,1)} %get-tuple-element.50), channel_id=1, source_target_pairs={{0,16},{16,32},{32,48},{48,64},{64,80},{80,96},{96,112},{112,0},{1... | collective-permute-start | bytes 786440 | tf_op jit(solution)/shard_map/ppermute | solution.py:21
  45.1 12.4 %collective-permute-start.6 = (bf16[32,2048]{1,0:T(8,128)(2,1)S(1)}, bf16[32,2048]{1,0:T(8,128)(2,1)S(1)}, u32[]{:S(2)}, u32[]{:S(2)}) collective-permute-start(bf16[32,2048]{1,0:T(8,128)(2,1)S(1)} %slice.48), channel_id=1, source_target_pairs={{0,32},{16,48},{32,64},{48,80},{64,96},{80,112},{96,0},{112,16},{1... | collective-permute-start | bytes 393224 | tf_op jit(solution)/shard_map/ppermute | solution.py:21
  45.9 12.8 %collective-permute-start.7 = (bf16[32,2048]{1,0:T(8,128)(2,1)S(1)}, bf16[32,2048]{1,0:T(8,128)(2,1)S(1)}, u32[]{:S(2)}, u32[]{:S(2)}) collective-permute-start(bf16[32,2048]{1,0:T(8,128)(2,1)S(1)} %slice.49), channel_id=1, source_target_pairs={{0,96},{16,112},{32,0},{48,16},{64,32},{80,48},{96,64},{112,80},{1... | collective-permute-start | bytes 393224 | tf_op jit(solution)/shard_map/ppermute | solution.py:21
  49.4 10.2 %collective-permute-start.5 = (bf16[64,2048]{1,0:T(8,128)(2,1)S(1)}, bf16[64,2048]{1,0:T(8,128)(2,1)S(1)}, u32[]{:S(2)}, u32[]{:S(2)}) collective-permute-start(bf16[64,2048]{1,0:T(8,128)(2,1)S(1)} %collective-permute-done.2), channel_id=1, source_target_pairs={{0,112},{16,0},{32,16},{48,32},{64,48},{80,64},{96,80},{112,96},{1... | collective-permute-start | bytes 786440 | tf_op jit(solution)/shard_map/ppermute | solution.py:21
  53.0 7.6 %collective-permute-start.8 = (bf16[64,2048]{1,0:T(8,128)(2,1)S(1)}, bf16[64,2048]{1,0:T(8,128)(2,1)S(1)}, u32[]{:S(2)}, u32[]{:S(2)}) collective-permute-start(bf16[64,2048]{1,0:T(8,128)(2,1)S(1)} %collective-permute-done.3), channel_id=1, source_target_pairs={{0,16},{16,32},{32,48},{48,64},{64,80},{80,96},{96,112},{112,0},{1... | collective-permute-start | bytes 786440 | tf_op jit(solution)/shard_map/ppermute | solution.py:21
  57.5 22.3 %collective-permute-start.11 = (bf16[1792,2,128]{2,1,0:T(2,128)(2,1)}, bf16[1792,2,128]{2,1,0:T(2,128)(2,1)}, u32[]{:S(2)}, u32[]{:S(2)}) collective-permute-start(bf16[1792,2,128]{2,1,0:T(2,128)(2,1)} %get-tuple-element.39), channel_id=1, source_target_pairs={{0,6},{2,0},{4,2},{6,4},{1,7},{3,1},{5,3},{7,5},{8,14},{10,8},{12,... | collective-permute-start | bytes 2752520 | tf_op jit(solution)/shard_map/ppermute | solution.py:21
  58.7 24.0 %collective-permute-start.9 = (bf16[1792,2,128]{2,1,0:T(2,128)(2,1)}, bf16[1792,2,128]{2,1,0:T(2,128)(2,1)}, u32[]{:S(2)}, u32[]{:S(2)}) collective-permute-start(bf16[1792,2,128]{2,1,0:T(2,128)(2,1)} %get-tuple-element.41), channel_id=1, source_target_pairs={{0,2},{2,4},{4,6},{6,0},{1,3},{3,5},{5,7},{7,1},{8,10},{10,12},{12... | collective-permute-start | bytes 2752520 | tf_op jit(solution)/shard_map/ppermute | solution.py:21
  62.7 28.3 %all-to-all-start = ((bf16[128,4,512]{2,1,0:T(4,128)(2,1)}), bf16[128,4,512]{2,1,0:T(4,128)(2,1)S(1)}, u32[]{:S(2)}, u32[]{:S(2)}) async-start(bf16[128,4,512]{2,1,0:T(4,128)(2,1)} %reshape.192), calls=%async_computation | async-start | bytes 1048576 | tf_op jit(solution)/shard_map/all_to_all | solution.py:160
  86.0 5.5 %copy-start.3 = (bf16[4,7168]{1,0:T(4,128)(2,1)S(1)}, bf16[4,7168]{1,0:T(4,128)(2,1)}, u32[]{:S(2)}) copy-start(bf16[4,7168]{1,0:T(4,128)(2,1)} %param.12) | copy-start | bytes 172036
  86.0 5.7 %copy-start.5 = (f32[7168]{0:T(1024)S(1)}, f32[7168]{0:T(1024)}, u32[]{:S(2)}) copy-start(f32[7168]{0:T(1024)} %param.18) | copy-start | bytes 86020
  128.9 7.8 %collective-permute-start.12 = (bf16[512,896]{1,0:T(8,128)(2,1)}, bf16[512,896]{1,0:T(8,128)(2,1)S(1)}, u32[]{:S(2)}, u32[]{:S(2)}) collective-permute-start(bf16[512,896]{1,0:T(8,128)(2,1)} %reshape.200), channel_id=1, source_target_pairs={{0,1},{1,0},{2,3},{3,2},{4,5},{5,4},{6,7},{7,6},{8,9},{9,8},{10,11... | collective-permute-start | bytes 2752520 | tf_op jit(solution)/shard_map/ppermute | solution.py:21
  128.9 5.4 %copy-start.1 = (bf16[1792,1024]{1,0:T(8,128)(2,1)S(1)}, bf16[1792,1024]{1,0:T(8,128)(2,1)}, u32[]{:S(2)}) copy-start(bf16[1792,1024]{1,0:T(8,128)(2,1)} %pad_maximum_fusion) | copy-start | bytes 11010052
  130.6 24.1 %collective-permute-start.19 = (bf16[128,1792]{1,0:T(8,128)(2,1)S(1)}, bf16[128,1792]{1,0:T(8,128)(2,1)S(1)}, u32[]{:S(2)}, u32[]{:S(2)}) collective-permute-start(bf16[128,1792]{1,0:T(8,128)(2,1)S(1)} %get-tuple-element.45), channel_id=1, source_target_pairs={{0,2},{2,4},{4,6},{6,0},{1,3},{3,5},{5,7},{7,1},{8,10},{10,12},{12... | collective-permute-start | bytes 1376264 | tf_op jit(solution)/shard_map/ppermute | solution.py:21
  131.3 23.4 %collective-permute-start.20 = (bf16[128,1792]{1,0:T(8,128)(2,1)S(1)}, bf16[128,1792]{1,0:T(8,128)(2,1)S(1)}, u32[]{:S(2)}, u32[]{:S(2)}) collective-permute-start(bf16[128,1792]{1,0:T(8,128)(2,1)S(1)} %get-tuple-element.44), channel_id=1, source_target_pairs={{0,4},{2,6},{4,0},{6,2},{1,5},{3,7},{5,1},{7,3},{8,12},{10,14},{12... | collective-permute-start | bytes 1376264 | tf_op jit(solution)/shard_map/ppermute | solution.py:21
  132.6 23.5 %collective-permute-start.21 = (bf16[128,1792]{1,0:T(8,128)(2,1)S(1)}, bf16[128,1792]{1,0:T(8,128)(2,1)S(1)}, u32[]{:S(2)}, u32[]{:S(2)}) collective-permute-start(bf16[128,1792]{1,0:T(8,128)(2,1)S(1)} %get-tuple-element.43), channel_id=1, source_target_pairs={{0,6},{2,0},{4,2},{6,4},{1,7},{3,1},{5,3},{7,5},{8,14},{10,8},{12,... | collective-permute-start | bytes 1376264 | tf_op jit(solution)/shard_map/ppermute | solution.py:21
  138.1 28.7 %collective-permute-start.14 = (bf16[512,256]{1,0:T(8,128)(2,1)S(1)}, bf16[512,256]{1,0:T(8,128)(2,1)S(1)}, u32[]{:S(2)}, u32[]{:S(2)}) collective-permute-start(bf16[512,256]{1,0:T(8,128)(2,1)S(1)} %get-tuple-element.49), channel_id=1, source_target_pairs={{0,6},{2,0},{4,2},{6,4},{1,7},{3,1},{5,3},{7,5},{8,14},{10,8},{12,... | collective-permute-start | bytes 786440 | tf_op jit(solution)/shard_map/ppermute | solution.py:21
  156.1 10.8 %collective-permute-start.13 = (bf16[512,256]{1,0:T(8,128)(2,1)S(1)}, bf16[512,256]{1,0:T(8,128)(2,1)S(1)}, u32[]{:S(2)}, u32[]{:S(2)}) collective-permute-start(bf16[512,256]{1,0:T(8,128)(2,1)S(1)} %get-tuple-element.47), channel_id=1, source_target_pairs={{0,4},{2,6},{4,0},{6,2},{1,5},{3,7},{5,1},{7,3},{8,12},{10,14},{12... | collective-permute-start | bytes 786440 | tf_op jit(solution)/shard_map/ppermute | solution.py:21
  157.1 13.0 %collective-permute-start.15 = (bf16[512,256]{1,0:T(8,128)(2,1)S(1)}, bf16[512,256]{1,0:T(8,128)(2,1)S(1)}, u32[]{:S(2)}, u32[]{:S(2)}) collective-permute-start(bf16[512,256]{1,0:T(8,128)(2,1)S(1)} %get-tuple-element.48), channel_id=1, source_target_pairs={{0,2},{2,4},{4,6},{6,0},{1,3},{3,5},{5,7},{7,1},{8,10},{10,12},{12... | collective-permute-start | bytes 786440 | tf_op jit(solution)/shard_map/ppermute | solution.py:21
  159.2 21.5 %collective-permute-start.23 = (bf16[512,896]{1,0:T(8,128)(2,1)S(1)}, bf16[512,896]{1,0:T(8,128)(2,1)S(1)}, u32[]{:S(2)}, u32[]{:S(2)}) collective-permute-start(bf16[512,896]{1,0:T(8,128)(2,1)S(1)} %constant_dynamic-slice_fusion), channel_id=1, source_target_pairs={{0,1},{1,0},{2,3},{3,2},{4,5},{5,4},{6,7},{7,6},{8,9},{9,8},{10,11... | collective-permute-start | bytes 2752520 | tf_op jit(solution)/shard_map/ppermute | solution.py:21
  170.4 9.5 %collective-permute-start.16 = (bf16[512,128]{1,0:T(8,128)(2,1)S(1)}, bf16[512,128]{1,0:T(8,128)(2,1)S(1)}, u32[]{:S(2)}, u32[]{:S(2)}) collective-permute-start(bf16[512,128]{1,0:T(8,128)(2,1)S(1)} %fusion.56), channel_id=1, source_target_pairs={{0,2},{2,4},{4,6},{6,0},{1,3},{3,5},{5,7},{7,1},{8,10},{10,12},{12... | collective-permute-start | bytes 393224 | tf_op jit(solution)/shard_map/ppermute | solution.py:21
  170.5 9.4 %collective-permute-start.17 = (bf16[512,128]{1,0:T(8,128)(2,1)S(1)}, bf16[512,128]{1,0:T(8,128)(2,1)S(1)}, u32[]{:S(2)}, u32[]{:S(2)}) collective-permute-start(bf16[512,128]{1,0:T(8,128)(2,1)S(1)} %fusion.56), channel_id=1, source_target_pairs={{0,4},{2,6},{4,0},{6,2},{1,5},{3,7},{5,1},{7,3},{8,12},{10,14},{12... | collective-permute-start | bytes 393224 | tf_op jit(solution)/shard_map/ppermute | solution.py:21
  172.5 8.0 %collective-permute-start.18 = (bf16[512,128]{1,0:T(8,128)(2,1)S(1)}, bf16[512,128]{1,0:T(8,128)(2,1)S(1)}, u32[]{:S(2)}, u32[]{:S(2)}) collective-permute-start(bf16[512,128]{1,0:T(8,128)(2,1)S(1)} %fusion.56), channel_id=1, source_target_pairs={{0,6},{2,0},{4,2},{6,4},{1,7},{3,1},{5,3},{7,5},{8,14},{10,8},{12,... | collective-permute-start | bytes 393224 | tf_op jit(solution)/shard_map/ppermute | solution.py:21
  180.6 2.0 collective-permute-start.22
  184.0 11.2 %copy-start.7 = (f32[4]{0:T(128)S(1)}, f32[4]{0:T(128)}, u32[]{:S(2)}) copy-start(f32[4]{0:T(128)} %get-tuple-element.59) | copy-start | bytes 52
  185.3 36.5 %copy-start.4 = (bf16[4,7168]{1,0:T(4,128)(2,1)S(1)}, bf16[4,7168]{1,0:T(4,128)(2,1)}, u32[]{:S(2)}) copy-start(bf16[4,7168]{1,0:T(4,128)(2,1)} %param.12) | copy-start | bytes 172036
  185.3 36.1 %all-to-all-start.2 = ((bf16[256,2,896]{2,1,0:T(2,128)(2,1)}), bf16[256,2,896]{2,1,0:T(2,128)(2,1)S(1)}, u32[]{:S(2)}, u32[]{:S(2)}) async-start(bf16[256,2,896]{2,1,0:T(2,128)(2,1)} %reshape.201), calls=%async_computation.2 | async-start | bytes 1835008 | tf_op jit(solution)/shard_map/all_to_all | solution.py:225
where the time goes:
time: 225 us; the launch traced here: 222 us
  waiting for transfers between devices  89.6 us (40%)
  starting transfers between devices  50.8 us (23%)
  blocking collectives  33.9 us (15%)
  local copies, waits for them, and re-layouts  24.7 us (11%)
  matrix products  16.1 us (7%)
  other arithmetic  6.27 us (3%)
    ppermute x24, waiting for transfers between devices, shifted(): return lax.ppermute(x, axis, [(i, (i + step) % size) for i in range(size)])  60.5 us
    ppermute x24, starting transfers between devices, shifted(): return lax.ppermute(x, axis, [(i, (i + step) % size) for i in range(size)])  34.1 us
    all_to_all x1, blocking collectives, layer(): lax.all_to_all(outgoing, SEC_GRP_TP, split_axis=0, concat_axis=0, tiled=T...  33.9 us
    all_to_all x1, waiting for transfers between devices, layer(): lax.all_to_all(values, SEC_GRP_TP, split_axis=0, concat_axis=0, tiled=True)  26.1 us
    all_to_all x1, starting transfers between devices, layer(): lax.all_to_all(values, SEC_GRP_TP, split_axis=0, concat_axis=0, tiled=True)  8.42 us
    all_to_all x1, starting transfers between devices, layer(): lax.all_to_all(partial_value, GRP_TP, split_axis=0, concat_axis=0, tiled=...  8.31 us
    unnamed x24, local copies, waits for them, and re-layouts  7.97 us
    dynamic_slice x1, local copies, waits for them, and re-layouts, layer(): lax.dynamic_slice_in_dim(expert_in[0], (chip + step) % chips * rows_of_ch...  4.94 us
  transfers between devices with their start and end apart: 26, of which 14 were waited for; matrix products, arithmetic and copies ran while one was open for 12% of the time, Pallas kernels for 0%

commit v1 on v0

--- a/solution.py
+++ b/solution.py
@@ -9,6 +9,7 @@
 SEC_GRP = ("sec", "grp_0", "grp_1")
 TP = ("x", "core")
 GRP_TP = ("grp_0", "grp_1", "x", "core")
+TP_SEC_GRP = ("x", "core", "sec", "grp_0", "grp_1")
 SEC_GRP_TP = ("sec", "grp_0", "grp_1", "x", "core")
 
 
@@ -185,16 +186,16 @@
         slot_index[:, :, None] == jnp.arange(capacity)[None, None, :]
     )
     outgoing = jnp.einsum(
-        "poy,ptj->otyj",
+        "poy,ptj->toyj",
         placed_tokens.astype(jnp.bfloat16),
         normalized_input.reshape(count_of_tokens, slices, part),
         preferred_element_type=jnp.float32,
     ).astype(jnp.bfloat16)
-    outgoing = outgoing.reshape(experts * slices, capacity, part)
+    outgoing = outgoing.reshape(slices * experts, capacity, part)
     outgoing, in_columns = lax.optimization_barrier((outgoing, in_columns))
     in_own, in_other = own_and_other(in_columns, core, 0)
     arrived_rows = lax.all_to_all(
-        outgoing, SEC_GRP_TP, split_axis=0, concat_axis=0, tiled=True
+        outgoing, TP_SEC_GRP, split_axis=0, concat_axis=0, tiled=True
     )
 
     rows = arrived_rows.reshape(-1, part)
@@ -221,9 +222,9 @@
         jnp.dot(hidden_own, out_own, preferred_element_type=jnp.float32)
         + jnp.dot(hidden_other, out_other, preferred_element_type=jnp.float32)
     ).astype(jnp.bfloat16)
-    values = values.reshape(experts * slices, capacity, part)
-    back = lax.all_to_all(values, SEC_GRP_TP, split_axis=0, concat_axis=0, tiled=True)
-    back = back.reshape(experts, slices, capacity, part)
+    values = values.reshape(slices * experts, capacity, part)
+    back = lax.all_to_all(values, TP_SEC_GRP, split_axis=0, concat_axis=0, tiled=True)
+    back = back.reshape(slices, experts, capacity, part)
 
     placed_late, _ = lax.optimization_barrier((placed_tokens, values))
     logits = jnp.dot(normalized_input, router, preferred_element_type=jnp.float32)
@@ -240,7 +241,7 @@
 
     coarse = lax.reduce_precision(combine_rows, 8, 7)
     weights = jnp.concatenate([coarse, combine_rows - coarse], axis=0).astype(jnp.bfloat16)
-    mixed = jnp.einsum("poy,otyj->ptj", weights, back, preferred_element_type=jnp.float32)
+    mixed = jnp.einsum("poy,toyj->ptj", weights, back, preferred_element_type=jnp.float32)
     expert_mix = (mixed[:count_of_tokens] + mixed[count_of_tokens:]).reshape(count_of_tokens, width)
     return (residual + expert_mix).astype(jnp.bfloat16)
 

time: 225 us -> 225 us (level)
  no operation moved by 1% of the time
where the time goes in v1:
time: 225 us; the launch traced here: 223 us
  waiting for transfers between devices  90.5 us (40%)
  starting transfers between devices  49.6 us (22%)
  blocking collectives  35.3 us (16%)
  local copies, waits for them, and re-layouts  24.2 us (11%)
  matrix products  16.1 us (7%)
  other arithmetic  6.27 us (3%)
    ppermute x24, waiting for transfers between devices, shifted(): return lax.ppermute(x, axis, [(i, (i + step) % size) for i in range(size)])  60.1 us
    all_to_all x1, blocking collectives, layer(): lax.all_to_all(outgoing, TP_SEC_GRP, split_axis=0, concat_axis=0, tiled=T...  35.3 us
    ppermute x24, starting transfers between devices, shifted(): return lax.ppermute(x, axis, [(i, (i + step) % size) for i in range(size)])  34.5 us
    all_to_all x1, waiting for transfers between devices, layer(): lax.all_to_all(values, TP_SEC_GRP, split_axis=0, concat_axis=0, tiled=True)  27.4 us
    all_to_all x1, starting transfers between devices, layer(): lax.all_to_all(partial_value, GRP_TP, split_axis=0, concat_axis=0, tiled=...  8.31 us
    unnamed x24, local copies, waits for them, and re-layouts  7.97 us
    all_to_all x1, starting transfers between devices, layer(): lax.all_to_all(values, TP_SEC_GRP, split_axis=0, concat_axis=0, tiled=True)  6.74 us
    dynamic_slice x1, local copies, waits for them, and re-layouts, layer(): lax.dynamic_slice_in_dim(expert_in[0], (chip + step) % chips * rows_of_ch...  4.94 us
  transfers between devices with their start and end apart: 26, of which 14 were waited for; matrix products, arithmetic and copies ran while one was open for 12% of the time, Pallas kernels for 0%

profile of v1, /device:TPU:8, one launch (start us, length us, event | category | flops | bytes accessed | tf_op | source)
XLA Modules:
  0.0 223.0 jit_solution(17877878601672127500)
XLA Ops:
  0.0 0.9 iota_compare_fusion.1
  0.9 2.9 %fusion.30 = f32[32,16,64]{2,1,0:T(8,128)S(1)} fusion(bf16[32,64,576]{2,1,0:T(8,128)(2,1)} %param.14, bf16[32,16,1,576]{3,1,2,0:T(8,128)(2,1)} %param.13, pred[32,64]{1,0:T(8,128)(4,1)S(1)} %iota_compare_fusion.1), kind=kOutput, calls=%fused_computation.26 | convolution fusion | flops 37814272 | bytes 3082240 | tf_op jit(solution)/shard_map/bhr,bpr->bhp/dot_general | solution.py:100
  4.0 2.5 %fusion.19 = bf16[32,16,512]{2,1,0:T(8,128)(2,1)S(1)} fusion(bf16[32,64,576]{2,1,0:T(8,128)(2,1)} %param.14, f32[32,16]{1,0:T(8,128)S(1)} %fusion.73, f32[32,16,64]{2,1,0:T(8,128)S(1)} %fusion.30), kind=kOutput, calls=%fused_computation.20 | convolution fusion | flops 33915456 | bytes 3162112 | tf_op jit(solution)/shard_map/bhp,bpc->bhc/dot_general | solution.py:109
  7.2 4.9 %dynamic-slice_bitcast_fusion = (bf16[1792,2,128]{2,1,0:T(2,128)(2,1)}, bf16[1792,2,128]{2,1,0:T(2,128)(2,1)}, bf16[1792,2,128]{2,1,0:T(2,128)(2,1)}, bf16[1792,2,128]{2,1,0:T(2,128)(2,1)S(1)}) fusion(bf16[1,7168,2,128]{3,2,1,0:T(2,128)(2,1)} %param.22, s32[]{:T(128)S(6)} %select_n.79, s32[]{:T(128)S(6)} %select_n.77, s32[]{:T(128)S(6)} %select_n.75, ...), kind=kLoop, calls=%fused_computation.44 | loop fusion | bytes 7340048 | tf_op jit(solution)/shard_map/dynamic_slice | solution.py:148
  12.2 3.0 %collective-permute-start.10 = (bf16[1792,2,128]{2,1,0:T(2,128)(2,1)}, bf16[1792,2,128]{2,1,0:T(2,128)(2,1)}, u32[]{:S(2)}, u32[]{:S(2)}) collective-permute-start(bf16[1792,2,128]{2,1,0:T(2,128)(2,1)} %get-tuple-element.40), channel_id=1, source_target_pairs={{0,4},{2,6},{4,0},{6,2},{1,5},{3,7},{5,1},{7,3},{8,12},{10,14},{12... | collective-permute-start | bytes 2752520 | tf_op jit(solution)/shard_map/ppermute | solution.py:22
  15.2 2.3 %collective-permute-start = (bf16[32,2048]{1,0:T(8,128)(2,1)S(1)}, bf16[32,2048]{1,0:T(8,128)(2,1)S(1)}, u32[]{:S(2)}, u32[]{:S(2)}) collective-permute-start(bf16[32,2048]{1,0:T(8,128)(2,1)S(1)} %bitcast.109), channel_id=1, source_target_pairs={{0,8},{8,0},{1,9},{9,1},{2,10},{10,2},{3,11},{11,3},{4,12},{12,4},... | collective-permute-start | bytes 393224 | tf_op jit(solution)/shard_map/ppermute | solution.py:22
  19.6 2.0 collective-permute-done
  22.4 5.9 %collective-permute-start.1 = (bf16[64,2048]{1,0:T(8,128)(2,1)}, bf16[64,2048]{1,0:T(8,128)(2,1)}, u32[]{:S(2)}, u32[]{:S(2)}) collective-permute-start(bf16[64,2048]{1,0:T(8,128)(2,1)} %get-tuple-element.50), channel_id=1, source_target_pairs={{0,112},{16,0},{32,16},{48,32},{64,48},{80,64},{96,80},{112,96},{1... | collective-permute-start | bytes 786440 | tf_op jit(solution)/shard_map/ppermute | solution.py:22
  28.3 1.4 collective-permute-start.2
  29.7 1.5 collective-permute-start.3
  31.2 3.9 %copy.47 = bf16[16,1,128,448]{2,0,3,1:T(8,128)(2,1)} copy(bf16[16,1,128,448]{2,3,1,0:T(8,128)(2,1)} %param.17) | data formatting | bytes 3670016 | tf_op args[5]
  35.2 9.8 %collective-permute-done.3 = bf16[64,2048]{1,0:T(8,128)(2,1)S(1)} collective-permute-done((bf16[64,2048]{1,0:T(8,128)(2,1)}, bf16[64,2048]{1,0:T(8,128)(2,1)S(1)}, u32[]{:S(2)}, u32[]{:S(2)}) %collective-permute-start.3) | collective-permute-done | bytes 262176 | tf_op jit(solution)/shard_map/ppermute | solution.py:22
  45.9 3.5 %collective-permute-start.7 = (bf16[32,2048]{1,0:T(8,128)(2,1)S(1)}, bf16[32,2048]{1,0:T(8,128)(2,1)S(1)}, u32[]{:S(2)}, u32[]{:S(2)}) collective-permute-start(bf16[32,2048]{1,0:T(8,128)(2,1)S(1)} %slice.49), channel_id=1, source_target_pairs={{0,96},{16,112},{32,0},{48,16},{64,32},{80,48},{96,64},{112,80},{1... | collective-permute-start | bytes 393224 | tf_op jit(solution)/shard_map/ppermute | solution.py:22
  49.8 1.7 constant_dynamic-update-slice_fusion.5
  53.0 1.6 collective-permute-start.8
  55.3 2.2 fusion.22
  57.5 1.2 collective-permute-start.11
  58.7 0.9 collective-permute-start.9
  59.7 0.9 collective-permute-done.8
  61.8 0.9 reshape.192
  62.7 8.3 %all-to-all-start = ((bf16[128,4,512]{2,1,0:T(4,128)(2,1)}), bf16[128,4,512]{2,1,0:T(4,128)(2,1)S(1)}, u32[]{:S(2)}, u32[]{:S(2)}) async-start(bf16[128,4,512]{2,1,0:T(4,128)(2,1)} %reshape.192), calls=%async_computation | async-start | bytes 1048576 | tf_op jit(solution)/shard_map/all_to_all | solution.py:161
  71.0 8.8 %collective-permute-done.11 = bf16[1792,2,128]{2,1,0:T(2,128)(2,1)} collective-permute-done((bf16[1792,2,128]{2,1,0:T(2,128)(2,1)}, bf16[1792,2,128]{2,1,0:T(2,128)(2,1)}, u32[]{:S(2)}, u32[]{:S(2)}) %collective-permute-start.11) | collective-permute-done | bytes 917536 | tf_op jit(solution)/shard_map/ppermute | solution.py:22
  79.8 2.9 %collective-permute-done.9 = bf16[1792,2,128]{2,1,0:T(2,128)(2,1)} collective-permute-done((bf16[1792,2,128]{2,1,0:T(2,128)(2,1)}, bf16[1792,2,128]{2,1,0:T(2,128)(2,1)}, u32[]{:S(2)}, u32[]{:S(2)}) %collective-permute-start.9) | collective-permute-done | bytes 917536 | tf_op jit(solution)/shard_map/ppermute | solution.py:22
  82.7 1.5 copy_bitcast_fusion.2
  84.2 1.7 copy_bitcast_fusion
  86.0 2.1 pad_maximum_fusion
  88.0 3.0 %all-to-all-done = bf16[128,4,512]{2,1,0:T(4,128)(2,1)S(1)} async-done(((bf16[128,4,512]{2,1,0:T(4,128)(2,1)}), bf16[128,4,512]{2,1,0:T(4,128)(2,1)S(1)}, u32[]{:S(2)}, u32[]{:S(2)}) %all-to-all-start) | async-done | bytes 524320 | tf_op jit(solution)/shard_map/all_to_all | solution.py:161
  92.3 0.9 copy.51
  93.3 35.3 %all_to_all.15 = bf16[256,2,896]{2,1,0:T(2,128)(2,1)S(1)} all-to-all(bf16[256,2,896]{2,1,0:T(2,128)(2,1)S(1)} %copy.51), channel_id=1, replica_groups=mesh['sec'=2,'grp_0'=8,'grp_1'=2,'x'=4,'core'=2] {'x','core','sec','grp_..., dimensions={0} | all-to-all | bytes 1835008 | tf_op jit(solution)/shard_map/all_to_all | solution.py:197
  128.5 1.3 reshape.200
  129.8 1.7 dynamic-slice_bitcast_fusion.4
  132.2 2.0 collective-permute-start.20
  135.0 2.4 %fusion.11 = f32[512,1024]{1,0:T(8,128)S(1)} fusion(bf16[512,896]{1,0:T(8,128)(2,1)} %reshape.200, bf16[1792,1024]{1,0:T(8,128)(2,1)S(1)} %copy-done.1, s32[]{:T(128)S(6)} %select_n.80), kind=kOutput, calls=%fused_computation.13 | convolution fusion | flops 939524096 | bytes 4849668 | tf_op jit(solution)/shard_map/dot_general | solution.py:203
  137.4 1.3 fusion.74
  138.8 1.4 collective-permute-start.14
  140.2 15.4 %collective-permute-done.19 = bf16[128,1792]{1,0:T(8,128)(2,1)S(1)} collective-permute-done((bf16[128,1792]{1,0:T(8,128)(2,1)S(1)}, bf16[128,1792]{1,0:T(8,128)(2,1)S(1)}, u32[]{:S(2)}, u32[]{:S(2)}) %collective-permute-start.19) | collective-permute-done | bytes 458784 | tf_op jit(solution)/shard_map/ppermute | solution.py:22
  155.6 1.4 collective-permute-done.21
  157.8 2.1 collective-permute-start.15
  160.2 7.6 %collective-permute-done.13 = bf16[512,256]{1,0:T(8,128)(2,1)S(1)} collective-permute-done((bf16[512,256]{1,0:T(8,128)(2,1)S(1)}, bf16[512,256]{1,0:T(8,128)(2,1)S(1)}, u32[]{:S(2)}, u32[]{:S(2)}) %collective-permute-start.13) | collective-permute-done | bytes 262176 | tf_op jit(solution)/shard_map/ppermute | solution.py:22
  167.8 3.2 %collective-permute-done.15 = bf16[512,256]{1,0:T(8,128)(2,1)S(1)} collective-permute-done((bf16[512,256]{1,0:T(8,128)(2,1)S(1)}, bf16[512,256]{1,0:T(8,128)(2,1)S(1)}, u32[]{:S(2)}, u32[]{:S(2)}) %collective-permute-start.15) | collective-permute-done | bytes 262176 | tf_op jit(solution)/shard_map/ppermute | solution.py:22
  171.4 2.1 collective-permute-start.17
  173.4 1.8 collective-permute-start.18
  175.3 5.5 %collective-permute-done.16 = bf16[512,128]{1,0:T(8,128)(2,1)S(1)} collective-permute-done((bf16[512,128]{1,0:T(8,128)(2,1)S(1)}, bf16[512,128]{1,0:T(8,128)(2,1)S(1)}, u32[]{:S(2)}, u32[]{:S(2)}) %collective-permute-start.16) | collective-permute-done | bytes 131104 | tf_op jit(solution)/shard_map/ppermute | solution.py:22
  181.5 1.9 collective-permute-done.22
  184.9 1.3 reshape.201
  186.2 6.7 %all-to-all-start.2 = ((bf16[256,2,896]{2,1,0:T(2,128)(2,1)}), bf16[256,2,896]{2,1,0:T(2,128)(2,1)S(1)}, u32[]{:S(2)}, u32[]{:S(2)}) async-start(bf16[256,2,896]{2,1,0:T(2,128)(2,1)} %reshape.201), calls=%async_computation.2 | async-start | bytes 1835008 | tf_op jit(solution)/shard_map/all_to_all | solution.py:226
  192.9 1.2 fusion.39
  194.5 27.4 %all-to-all-done.2 = bf16[256,2,896]{2,1,0:T(2,128)(2,1)S(1)} async-done(((bf16[256,2,896]{2,1,0:T(2,128)(2,1)}), bf16[256,2,896]{2,1,0:T(2,128)(2,1)S(1)}, u32[]{:S(2)}, u32[]{:S(2)}) %all-to-all-start.2) | async-done | bytes 917536 | tf_op jit(solution)/shard_map/all_to_all | solution.py:226
  (89 shorter events, 15.6 us)
Async XLA Ops:
  0.0 6.5 %copy-start = (bf16[16,1,512,128]{3,2,1,0:T(8,128)(2,1)S(1)}, bf16[16,1,512,128]{3,2,1,0:T(8,128)(2,1)}, u32[]{:S(2)}) copy-start(bf16[16,1,512,128]{3,2,1,0:T(8,128)(2,1)} %param.16) | copy-start | bytes 6291460
  7.2 11.4 %copy-start.6 = (s32[4,8]{1,0:T(4,128)S(1)}, s32[4,8]{1,0:T(4,128)}, u32[]{:S(2)}) copy-start(s32[4,8]{1,0:T(4,128)} %param.20) | copy-start | bytes 388
  12.2 58.9 %collective-permute-start.10 = (bf16[1792,2,128]{2,1,0:T(2,128)(2,1)}, bf16[1792,2,128]{2,1,0:T(2,128)(2,1)}, u32[]{:S(2)}, u32[]{:S(2)}) collective-permute-start(bf16[1792,2,128]{2,1,0:T(2,128)(2,1)} %get-tuple-element.40), channel_id=1, source_target_pairs={{0,4},{2,6},{4,0},{6,2},{1,5},{3,7},{5,1},{7,3},{8,12},{10,14},{12... | collective-permute-start | bytes 2752520 | tf_op jit(solution)/shard_map/ppermute | solution.py:22
  15.2 6.5 %collective-permute-start = (bf16[32,2048]{1,0:T(8,128)(2,1)S(1)}, bf16[32,2048]{1,0:T(8,128)(2,1)S(1)}, u32[]{:S(2)}, u32[]{:S(2)}) collective-permute-start(bf16[32,2048]{1,0:T(8,128)(2,1)S(1)} %bitcast.109), channel_id=1, source_target_pairs={{0,8},{8,0},{1,9},{9,1},{2,10},{10,2},{3,11},{11,3},{4,12},{12,4},... | collective-permute-start | bytes 393224 | tf_op jit(solution)/shard_map/ppermute | solution.py:22
  22.4 27.0 %collective-permute-start.1 = (bf16[64,2048]{1,0:T(8,128)(2,1)}, bf16[64,2048]{1,0:T(8,128)(2,1)}, u32[]{:S(2)}, u32[]{:S(2)}) collective-permute-start(bf16[64,2048]{1,0:T(8,128)(2,1)} %get-tuple-element.50), channel_id=1, source_target_pairs={{0,112},{16,0},{32,16},{48,32},{64,48},{80,64},{96,80},{112,96},{1... | collective-permute-start | bytes 786440 | tf_op jit(solution)/shard_map/ppermute | solution.py:22
  28.3 17.7 %collective-permute-start.2 = (bf16[64,2048]{1,0:T(8,128)(2,1)}, bf16[64,2048]{1,0:T(8,128)(2,1)S(1)}, u32[]{:S(2)}, u32[]{:S(2)}) collective-permute-start(bf16[64,2048]{1,0:T(8,128)(2,1)} %get-tuple-element.50), channel_id=1, source_target_pairs={{0,96},{16,112},{32,0},{48,16},{64,32},{80,48},{96,64},{112,80},{1... | collective-permute-start | bytes 786440 | tf_op jit(solution)/shard_map/ppermute | solution.py:22
  29.7 15.4 %collective-permute-start.3 = (bf16[64,2048]{1,0:T(8,128)(2,1)}, bf16[64,2048]{1,0:T(8,128)(2,1)S(1)}, u32[]{:S(2)}, u32[]{:S(2)}) collective-permute-start(bf16[64,2048]{1,0:T(8,128)(2,1)} %get-tuple-element.50), channel_id=1, source_target_pairs={{0,32},{16,48},{32,64},{48,80},{64,96},{80,112},{96,0},{112,16},{1... | collective-permute-start | bytes 786440 | tf_op jit(solution)/shard_map/ppermute | solution.py:22
  35.1 20.2 %copy-start.2 = (bf16[16,1,128,448]{2,0,3,1:T(8,128)(2,1)S(1)}, bf16[16,1,128,448]{2,0,3,1:T(8,128)(2,1)}, u32[]{:S(2)}) copy-start(bf16[16,1,128,448]{2,0,3,1:T(8,128)(2,1)} %copy.47) | copy-start | bytes 5505028
  35.2 17.8 %collective-permute-start.4 = (bf16[64,2048]{1,0:T(8,128)(2,1)}, bf16[64,2048]{1,0:T(8,128)(2,1)S(1)}, u32[]{:S(2)}, u32[]{:S(2)}) collective-permute-start(bf16[64,2048]{1,0:T(8,128)(2,1)} %get-tuple-element.50), channel_id=1, source_target_pairs={{0,16},{16,32},{32,48},{48,64},{64,80},{80,96},{96,112},{112,0},{1... | collective-permute-start | bytes 786440 | tf_op jit(solution)/shard_map/ppermute | solution.py:22
  45.1 12.4 %collective-permute-start.6 = (bf16[32,2048]{1,0:T(8,128)(2,1)S(1)}, bf16[32,2048]{1,0:T(8,128)(2,1)S(1)}, u32[]{:S(2)}, u32[]{:S(2)}) collective-permute-start(bf16[32,2048]{1,0:T(8,128)(2,1)S(1)} %slice.48), channel_id=1, source_target_pairs={{0,32},{16,48},{32,64},{48,80},{64,96},{80,112},{96,0},{112,16},{1... | collective-permute-start | bytes 393224 | tf_op jit(solution)/shard_map/ppermute | solution.py:22
  45.9 12.8 %collective-permute-start.7 = (bf16[32,2048]{1,0:T(8,128)(2,1)S(1)}, bf16[32,2048]{1,0:T(8,128)(2,1)S(1)}, u32[]{:S(2)}, u32[]{:S(2)}) collective-permute-start(bf16[32,2048]{1,0:T(8,128)(2,1)S(1)} %slice.49), channel_id=1, source_target_pairs={{0,96},{16,112},{32,0},{48,16},{64,32},{80,48},{96,64},{112,80},{1... | collective-permute-start | bytes 393224 | tf_op jit(solution)/shard_map/ppermute | solution.py:22
  49.4 10.2 %collective-permute-start.5 = (bf16[64,2048]{1,0:T(8,128)(2,1)S(1)}, bf16[64,2048]{1,0:T(8,128)(2,1)S(1)}, u32[]{:S(2)}, u32[]{:S(2)}) collective-permute-start(bf16[64,2048]{1,0:T(8,128)(2,1)S(1)} %collective-permute-done.2), channel_id=1, source_target_pairs={{0,112},{16,0},{32,16},{48,32},{64,48},{80,64},{96,80},{112,96},{1... | collective-permute-start | bytes 786440 | tf_op jit(solution)/shard_map/ppermute | solution.py:22
  53.0 7.6 %collective-permute-start.8 = (bf16[64,2048]{1,0:T(8,128)(2,1)S(1)}, bf16[64,2048]{1,0:T(8,128)(2,1)S(1)}, u32[]{:S(2)}, u32[]{:S(2)}) collective-permute-start(bf16[64,2048]{1,0:T(8,128)(2,1)S(1)} %collective-permute-done.3), channel_id=1, source_target_pairs={{0,16},{16,32},{32,48},{48,64},{64,80},{80,96},{96,112},{112,0},{1... | collective-permute-start | bytes 786440 | tf_op jit(solution)/shard_map/ppermute | solution.py:22
  57.5 22.3 %collective-permute-start.11 = (bf16[1792,2,128]{2,1,0:T(2,128)(2,1)}, bf16[1792,2,128]{2,1,0:T(2,128)(2,1)}, u32[]{:S(2)}, u32[]{:S(2)}) collective-permute-start(bf16[1792,2,128]{2,1,0:T(2,128)(2,1)} %get-tuple-element.39), channel_id=1, source_target_pairs={{0,6},{2,0},{4,2},{6,4},{1,7},{3,1},{5,3},{7,5},{8,14},{10,8},{12,... | collective-permute-start | bytes 2752520 | tf_op jit(solution)/shard_map/ppermute | solution.py:22
  58.7 24.0 %collective-permute-start.9 = (bf16[1792,2,128]{2,1,0:T(2,128)(2,1)}, bf16[1792,2,128]{2,1,0:T(2,128)(2,1)}, u32[]{:S(2)}, u32[]{:S(2)}) collective-permute-start(bf16[1792,2,128]{2,1,0:T(2,128)(2,1)} %get-tuple-element.41), channel_id=1, source_target_pairs={{0,2},{2,4},{4,6},{6,0},{1,3},{3,5},{5,7},{7,1},{8,10},{10,12},{12... | collective-permute-start | bytes 2752520 | tf_op jit(solution)/shard_map/ppermute | solution.py:22
  62.7 28.3 %all-to-all-start = ((bf16[128,4,512]{2,1,0:T(4,128)(2,1)}), bf16[128,4,512]{2,1,0:T(4,128)(2,1)S(1)}, u32[]{:S(2)}, u32[]{:S(2)}) async-start(bf16[128,4,512]{2,1,0:T(4,128)(2,1)} %reshape.192), calls=%async_computation | async-start | bytes 1048576 | tf_op jit(solution)/shard_map/all_to_all | solution.py:161
  86.0 5.5 %copy-start.3 = (bf16[4,7168]{1,0:T(4,128)(2,1)S(1)}, bf16[4,7168]{1,0:T(4,128)(2,1)}, u32[]{:S(2)}) copy-start(bf16[4,7168]{1,0:T(4,128)(2,1)} %param.12) | copy-start | bytes 172036
  86.0 5.7 %copy-start.5 = (f32[7168]{0:T(1024)S(1)}, f32[7168]{0:T(1024)}, u32[]{:S(2)}) copy-start(f32[7168]{0:T(1024)} %param.18) | copy-start | bytes 86020
  129.8 7.6 %collective-permute-start.12 = (bf16[512,896]{1,0:T(8,128)(2,1)}, bf16[512,896]{1,0:T(8,128)(2,1)S(1)}, u32[]{:S(2)}, u32[]{:S(2)}) collective-permute-start(bf16[512,896]{1,0:T(8,128)(2,1)} %reshape.200), channel_id=1, source_target_pairs={{0,1},{1,0},{2,3},{3,2},{4,5},{5,4},{6,7},{7,6},{8,9},{9,8},{10,11... | collective-permute-start | bytes 2752520 | tf_op jit(solution)/shard_map/ppermute | solution.py:22
  129.8 5.1 %copy-start.1 = (bf16[1792,1024]{1,0:T(8,128)(2,1)S(1)}, bf16[1792,1024]{1,0:T(8,128)(2,1)}, u32[]{:S(2)}) copy-start(bf16[1792,1024]{1,0:T(8,128)(2,1)} %pad_maximum_fusion) | copy-start | bytes 11010052
  131.5 24.1 %collective-permute-start.19 = (bf16[128,1792]{1,0:T(8,128)(2,1)S(1)}, bf16[128,1792]{1,0:T(8,128)(2,1)S(1)}, u32[]{:S(2)}, u32[]{:S(2)}) collective-permute-start(bf16[128,1792]{1,0:T(8,128)(2,1)S(1)} %get-tuple-element.45), channel_id=1, source_target_pairs={{0,2},{2,4},{4,6},{6,0},{1,3},{3,5},{5,7},{7,1},{8,10},{10,12},{12... | collective-permute-start | bytes 1376264 | tf_op jit(solution)/shard_map/ppermute | solution.py:22
  132.2 23.4 %collective-permute-start.20 = (bf16[128,1792]{1,0:T(8,128)(2,1)S(1)}, bf16[128,1792]{1,0:T(8,128)(2,1)S(1)}, u32[]{:S(2)}, u32[]{:S(2)}) collective-permute-start(bf16[128,1792]{1,0:T(8,128)(2,1)S(1)} %get-tuple-element.44), channel_id=1, source_target_pairs={{0,4},{2,6},{4,0},{6,2},{1,5},{3,7},{5,1},{7,3},{8,12},{10,14},{12... | collective-permute-start | bytes 1376264 | tf_op jit(solution)/shard_map/ppermute | solution.py:22
  134.2 22.7 %collective-permute-start.21 = (bf16[128,1792]{1,0:T(8,128)(2,1)S(1)}, bf16[128,1792]{1,0:T(8,128)(2,1)S(1)}, u32[]{:S(2)}, u32[]{:S(2)}) collective-permute-start(bf16[128,1792]{1,0:T(8,128)(2,1)S(1)} %get-tuple-element.43), channel_id=1, source_target_pairs={{0,6},{2,0},{4,2},{6,4},{1,7},{3,1},{5,3},{7,5},{8,14},{10,8},{12,... | collective-permute-start | bytes 1376264 | tf_op jit(solution)/shard_map/ppermute | solution.py:22
  138.8 29.0 %collective-permute-start.14 = (bf16[512,256]{1,0:T(8,128)(2,1)S(1)}, bf16[512,256]{1,0:T(8,128)(2,1)S(1)}, u32[]{:S(2)}, u32[]{:S(2)}) collective-permute-start(bf16[512,256]{1,0:T(8,128)(2,1)S(1)} %get-tuple-element.49), channel_id=1, source_target_pairs={{0,6},{2,0},{4,2},{6,4},{1,7},{3,1},{5,3},{7,5},{8,14},{10,8},{12,... | collective-permute-start | bytes 786440 | tf_op jit(solution)/shard_map/ppermute | solution.py:22
  157.0 10.8 %collective-permute-start.13 = (bf16[512,256]{1,0:T(8,128)(2,1)S(1)}, bf16[512,256]{1,0:T(8,128)(2,1)S(1)}, u32[]{:S(2)}, u32[]{:S(2)}) collective-permute-start(bf16[512,256]{1,0:T(8,128)(2,1)S(1)} %get-tuple-element.47), channel_id=1, source_target_pairs={{0,4},{2,6},{4,0},{6,2},{1,5},{3,7},{5,1},{7,3},{8,12},{10,14},{12... | collective-permute-start | bytes 786440 | tf_op jit(solution)/shard_map/ppermute | solution.py:22
  157.8 13.2 %collective-permute-start.15 = (bf16[512,256]{1,0:T(8,128)(2,1)S(1)}, bf16[512,256]{1,0:T(8,128)(2,1)S(1)}, u32[]{:S(2)}, u32[]{:S(2)}) collective-permute-start(bf16[512,256]{1,0:T(8,128)(2,1)S(1)} %get-tuple-element.48), channel_id=1, source_target_pairs={{0,2},{2,4},{4,6},{6,0},{1,3},{3,5},{5,7},{7,1},{8,10},{10,12},{12... | collective-permute-start | bytes 786440 | tf_op jit(solution)/shard_map/ppermute | solution.py:22
  160.1 21.4 %collective-permute-start.23 = (bf16[512,896]{1,0:T(8,128)(2,1)S(1)}, bf16[512,896]{1,0:T(8,128)(2,1)S(1)}, u32[]{:S(2)}, u32[]{:S(2)}) collective-permute-start(bf16[512,896]{1,0:T(8,128)(2,1)S(1)} %constant_dynamic-slice_fusion), channel_id=1, source_target_pairs={{0,1},{1,0},{2,3},{3,2},{4,5},{5,4},{6,7},{7,6},{8,9},{9,8},{10,11... | collective-permute-start | bytes 2752520 | tf_op jit(solution)/shard_map/ppermute | solution.py:22
  171.3 9.5 %collective-permute-start.16 = (bf16[512,128]{1,0:T(8,128)(2,1)S(1)}, bf16[512,128]{1,0:T(8,128)(2,1)S(1)}, u32[]{:S(2)}, u32[]{:S(2)}) collective-permute-start(bf16[512,128]{1,0:T(8,128)(2,1)S(1)} %fusion.56), channel_id=1, source_target_pairs={{0,2},{2,4},{4,6},{6,0},{1,3},{3,5},{5,7},{7,1},{8,10},{10,12},{12... | collective-permute-start | bytes 393224 | tf_op jit(solution)/shard_map/ppermute | solution.py:22
  171.4 9.4 %collective-permute-start.17 = (bf16[512,128]{1,0:T(8,128)(2,1)S(1)}, bf16[512,128]{1,0:T(8,128)(2,1)S(1)}, u32[]{:S(2)}, u32[]{:S(2)}) collective-permute-start(bf16[512,128]{1,0:T(8,128)(2,1)S(1)} %fusion.56), channel_id=1, source_target_pairs={{0,4},{2,6},{4,0},{6,2},{1,5},{3,7},{5,1},{7,3},{8,12},{10,14},{12... | collective-permute-start | bytes 393224 | tf_op jit(solution)/shard_map/ppermute | solution.py:22
  173.4 7.9 %collective-permute-start.18 = (bf16[512,128]{1,0:T(8,128)(2,1)S(1)}, bf16[512,128]{1,0:T(8,128)(2,1)S(1)}, u32[]{:S(2)}, u32[]{:S(2)}) collective-permute-start(bf16[512,128]{1,0:T(8,128)(2,1)S(1)} %fusion.56), channel_id=1, source_target_pairs={{0,6},{2,0},{4,2},{6,4},{1,7},{3,1},{5,3},{7,5},{8,14},{10,8},{12,... | collective-permute-start | bytes 393224 | tf_op jit(solution)/shard_map/ppermute | solution.py:22
  181.4 2.0 collective-permute-start.22
  184.9 9.5 %copy-start.7 = (f32[4]{0:T(128)S(1)}, f32[4]{0:T(128)}, u32[]{:S(2)}) copy-start(f32[4]{0:T(128)} %get-tuple-element.59) | copy-start | bytes 52
  186.1 36.2 %copy-start.4 = (bf16[4,7168]{1,0:T(4,128)(2,1)S(1)}, bf16[4,7168]{1,0:T(4,128)(2,1)}, u32[]{:S(2)}) copy-start(bf16[4,7168]{1,0:T(4,128)(2,1)} %param.12) | copy-start | bytes 172036
  186.2 35.8 %all-to-all-start.2 = ((bf16[256,2,896]{2,1,0:T(2,128)(2,1)}), bf16[256,2,896]{2,1,0:T(2,128)(2,1)S(1)}, u32[]{:S(2)}, u32[]{:S(2)}) async-start(bf16[256,2,896]{2,1,0:T(2,128)(2,1)} %reshape.201), calls=%async_computation.2 | async-start | bytes 1835008 | tf_op jit(solution)/shard_map/all_to_all | solution.py:226
